TPU v7x, 32 devices: a whole 2x2x4 slice. The times are simulated.
32 devices in a mesh: wide: 8 (over z, x), narrow: 4 (over y, core).
Axes of the slice: x: 2, y: 2, z: 4, core: 2. Of those that a mesh axis runs over, the one named last changes fastest.
Arguments:
- state: float32 [2, 2097152], P(None, ('wide', 'narrow')), may hold values from -6 to 6
- gates: float32 [8, 2, 128, 128], replicated, may hold values from -1 to 1, as said below
- gate_qubits: int32 [8, 7], replicated, may hold values from 7 to 15, as said below
- swap_order: int32 [9], replicated, may hold values from 7 to 15, as said below
Outputs:
- checkpoint: float32 [2, 2097152], P(None, ('wide', 'narrow'))
Inputs may be any that keep to these rules, and one draw needn't show every extreme that they name: `gate_qubits`: each row names 7 different qubits. `swap_order`: each number of the range appears once. Each gates[g, 0] + i gates[g, 1] is a unitary matrix.
All inputs are finite; a program needn't handle non-finite values.
Results may differ from a plain program's by a relative error of at most 0.0003.
Values sent between devices are 32-bit elements; how exact they have to be, the bound alone decides.
A program may use at most 64 MiB of HBM per device.

v0:
```python
import functools
import math

import jax
import jax.numpy as jnp
from jax import lax
from jax.experimental import pallas as pl
from jax.experimental.pallas import tpu as pltpu
from jax.sharding import PartitionSpec as P

LANE_QUBITS = 7
LANES = 2**LANE_QUBITS
CHUNKS = 2

companding = 16.0
companding_norm = math.log(16.0 + math.sqrt(257.0))

MESH = pl.DeviceIdType.MESH


def kernel(
    n_wide,
    n_narrow,
    upper,
    gate_bits,
    stages,
    qubits_hbm,
    swap_hbm,
    state_ref,
    gates_ref,
    out_ref,
    qubits_ref,
    swap_ref,
    state_v,
    gates_v,
    perms,
    mats,
    wide_out,
    wide_in,
    narrow_out,
    narrow_in,
    ext_out,
    ext_in,
    local_sem,
    gate_sem,
    wide_send,
    wide_recv,
    narrow_send,
    narrow_recv,
    ext_send,
    ext_recv,
):
    rows = 2**upper
    gate_dim = 2**gate_bits
    rest = rows // gate_dim
    wide_bits = n_wide.bit_length() - 1
    narrow_bits = n_narrow.bit_length() - 1
    wide_me = lax.axis_index("wide")
    narrow_me = lax.axis_index("narrow")
    half = LANES // 2

    qubits_copy = pltpu.make_async_copy(qubits_hbm, qubits_ref, local_sem.at[1])
    qubits_copy.start()
    swap_copy = pltpu.make_async_copy(swap_hbm, swap_ref, local_sem.at[2])
    swap_copy.start()
    state_copy = pltpu.make_async_copy(state_ref, state_v, local_sem.at[0])
    state_copy.start()
    gate_copies = []
    for number in range(gates_v.shape[0]):
        copy = pltpu.make_async_copy(
            gates_ref.at[number], gates_v.at[number], gate_sem.at[number]
        )
        copy.start()
        gate_copies.append(copy)

    barrier = pltpu.get_barrier_semaphore()
    devices = n_wide * n_narrow
    flat_me = wide_me * n_narrow + narrow_me

    def device_at(apart):
        other = lax.rem(flat_me + apart, devices)
        return (lax.div(other, n_narrow), lax.rem(other, n_narrow))

    def for_others(step):
        if devices <= 64:
            for apart in range(1, devices):
                step(apart)
        else:
            lax.fori_loop(1, devices, lambda apart, _: step(apart), None)

    def greet(apart):
        pl.semaphore_signal(barrier, inc=1, device_id=device_at(apart), device_id_type=MESH)

    for_others(greet)
    qubits_copy.wait()
    swap_copy.wait()

    def gate_layout(number):
        masks = [jnp.int32(1) << (qubits_ref[number, k] - LANE_QUBITS) for k in range(gate_bits)]
        left = jnp.int32(rows - 1)
        for mask in masks:
            left = left - mask
        for _ in range(upper - gate_bits):
            low = left & (-left)
            masks.append(low)
            left = left - low
        return masks

    def swap_layout(order):
        return [jnp.int32(1) << (swap_ref[k] - LANE_QUBITS) for k in order]

    natural = [jnp.int32(1 << k) for k in range(upper)]
    wide_layout = swap_layout(range(upper))
    narrow_layout = swap_layout(list(range(narrow_bits, upper)) + list(range(narrow_bits)))

    column = lax.broadcasted_iota(jnp.int32, (1, rows), 1)
    row = lax.broadcasted_iota(jnp.int32, (rows, rows), 0)

    def make_perm(slot, source, target):
        index = jnp.zeros((1, rows), jnp.int32)
        for k in range(upper):
            index = index + jnp.where((column & (1 << k)) != 0, source[k], 0)
        goal = jnp.zeros((1, rows), jnp.int32)
        for k in range(upper):
            goal = goal + jnp.where((index & target[k]) != 0, 1 << k, 0)
        perms[slot] = (row == goal).astype(jnp.float32).astype(jnp.bfloat16)

    def make_matrix(number):
        gate_copies[number].wait()
        whole = jnp.concatenate([gates_v[number, 0], gates_v[number, 1]], axis=1)
        high = whole.astype(jnp.bfloat16)
        low = (whole - high.astype(jnp.float32)).astype(jnp.bfloat16)
        mats[number, :gate_dim] = high
        mats[number, gate_dim:] = low

    sign = jnp.where(lax.broadcasted_iota(jnp.int32, (1, LANES), 1) < half, -1.0, 1.0)

    def permuted(values, slot):
        high = values.astype(jnp.bfloat16)
        low = (values - high.astype(jnp.float32)).astype(jnp.bfloat16)
        both = jnp.concatenate([high, low], axis=1)
        moved = jnp.dot(perms[slot], both, preferred_element_type=jnp.float32)
        return moved[:, :LANES], moved[:, LANES:]

    def gate(values, slot, number):
        both = jnp.concatenate(permuted(values, slot), axis=1)
        blocks = []
        for k in range(rest):
            part = both[k * gate_dim : (k + 1) * gate_dim]
            turned = jnp.concatenate(
                [
                    pltpu.roll(part[:, :LANES], half, 1) * sign,
                    pltpu.roll(part[:, LANES:], half, 1) * sign,
                ],
                axis=1,
            )
            whole = jnp.concatenate([part, turned], axis=0).astype(jnp.bfloat16)
            mixed = jnp.dot(mats[number], whole, preferred_element_type=jnp.float32)
            blocks.append(
                mixed[:gate_dim, :LANES]
                + (mixed[gate_dim:, :LANES] + mixed[:gate_dim, LANES:])
            )
        return jnp.concatenate(blocks, axis=0)

    def moved(values, slot):
        high, low = permuted(values, slot)
        return high + low

    def wide_copy(chunk, apart):
        other = lax.rem(wide_me + apart, n_wide)
        return pltpu.make_async_remote_copy(
            src_ref=wide_out.at[chunk, other],
            dst_ref=wide_in.at[chunk, wide_me],
            send_sem=wide_send.at[chunk, apart - 1],
            recv_sem=wide_recv.at[chunk, apart - 1],
            device_id=(other, narrow_me),
            device_id_type=MESH,
        )

    def narrow_copy(chunk, apart):
        other = lax.rem(narrow_me + apart, n_narrow)
        return pltpu.make_async_remote_copy(
            src_ref=narrow_out.at[chunk, other],
            dst_ref=narrow_in.at[chunk, narrow_me],
            send_sem=narrow_send.at[chunk, apart - 1],
            recv_sem=narrow_recv.at[chunk, apart - 1],
            device_id=(wide_me, other),
            device_id_type=MESH,
        )

    slot = 0
    plan = []
    for numbers, leave in zip(stages, (wide_layout, narrow_layout, natural)):
        plan.append((slot, numbers, leave))
        slot += len(numbers) + 1

    def prepare(stage, layout):
        start, numbers, leave = plan[stage]
        for k, number in enumerate(numbers):
            target = gate_layout(number)
            make_perm(start + k, layout, target)
            make_matrix(number)
            layout = target
        make_perm(start + len(numbers), layout, leave)

    def run(values, stage):
        start, numbers, _ = plan[stage]
        for k, number in enumerate(numbers):
            values = gate(values, start + k, number)
        return moved(values, start + len(numbers))

    prepare(0, natural)
    state_copy.wait()
    real = state_v[pl.ds(0, rows, stride=2), :]
    imag = state_v[pl.ds(1, rows, stride=2), :]
    first_half = lax.broadcasted_iota(jnp.int32, (1, LANES), 1) < half
    pieces = (
        jnp.where(first_half, real, pltpu.roll(imag, half, 1)),
        jnp.where(first_half, pltpu.roll(real, half, 1), imag),
    )
    for chunk in range(CHUNKS):
        values = run(pieces[chunk], 0)
        wide_out[chunk] = values.reshape(n_wide, rows // n_wide, LANES)
        if chunk == 0:
            pl.semaphore_wait(barrier, devices - 1)
        for apart in range(1, n_wide):
            wide_copy(chunk, apart).start()
        wide_in[chunk, wide_me] = wide_out[chunk, wide_me]

    prepare(1, wide_layout)
    prepare(2, narrow_layout)
    for chunk in range(CHUNKS):
        for apart in range(1, n_wide):
            wide_copy(chunk, apart).wait_recv()
        values = run(wide_in[chunk].reshape(rows, LANES), 1)
        narrow_out[chunk] = values.reshape(n_narrow, rows // n_narrow, LANES)
        for apart in range(1, n_narrow):
            narrow_copy(chunk, apart).start()
        narrow_in[chunk, narrow_me] = narrow_out[chunk, narrow_me]

    results = []
    for chunk in range(CHUNKS):
        for apart in range(1, n_narrow):
            narrow_copy(chunk, apart).wait_recv()
        results.append(run(narrow_in[chunk].reshape(rows, LANES), 2))

    high = jnp.maximum(results[0], results[1]).max(axis=0, keepdims=True)
    low = -jnp.minimum(results[0], results[1]).min(axis=0, keepdims=True)
    high = jnp.maximum(high, pltpu.roll(high, half, 1))
    low = jnp.maximum(low, pltpu.roll(low, half, 1))
    ext_out[...] = jnp.where(first_half, high, low)

    def ext_copy(apart):
        return pltpu.make_async_remote_copy(
            src_ref=ext_out,
            dst_ref=ext_in.at[apart - 1],
            send_sem=ext_send.at[apart - 1],
            recv_sem=ext_recv.at[apart - 1],
            device_id=device_at(apart),
            device_id_type=MESH,
        )

    for_others(lambda apart: ext_copy(apart).start())
    state_v[:rows] = jnp.where(first_half, results[0], pltpu.roll(results[1], half, 1))
    state_v[rows:] = jnp.where(first_half, pltpu.roll(results[0], half, 1), results[1])
    for chunk in range(CHUNKS):
        for apart in range(1, n_wide):
            wide_copy(chunk, apart).wait_send()
        for apart in range(1, n_narrow):
            narrow_copy(chunk, apart).wait_send()
    for_others(lambda apart: ext_copy(apart).wait_recv())
    total = jnp.maximum(ext_out[...], ext_in[...].max(axis=0))
    highest = jnp.max(jnp.where(first_half, total, -jnp.inf), axis=1, keepdims=True)
    lowest = -jnp.max(jnp.where(first_half, -jnp.inf, total), axis=1, keepdims=True)
    middle = (highest + lowest) * 0.5
    halfwidth = (highest - lowest) * 0.5 + 1e-06
    scale = companding / halfwidth
    for plane in range(2):
        values = (state_v[plane * rows : (plane + 1) * rows] - middle) * scale
        magnitude = jnp.abs(values)
        squared = magnitude * magnitude + 1.0
        grown = jnp.log(magnitude + squared * lax.rsqrt(squared)) * (1.0 / companding_norm)
        out_ref[pl.ds(plane, rows, stride=2), :] = jnp.where(values < 0, -grown, grown)
    for_others(lambda apart: ext_copy(apart).wait_send())


def local(state, gates, gate_qubits, swap_order):
    n_wide = lax.axis_size("wide")
    n_narrow = lax.axis_size("narrow")
    upper = state.shape[1].bit_length() - 1 - LANE_QUBITS
    rows = 2**upper
    gate_count, gate_bits = gate_qubits.shape
    gate_dim = 2**gate_bits
    stages = (range(3), range(3, 6), range(6, gate_count))
    dma = pltpu.SemaphoreType.DMA
    woven = state.reshape(2, rows, LANES).transpose(1, 0, 2).reshape(2 * rows, LANES)
    final = pl.pallas_call(
        functools.partial(kernel, n_wide, n_narrow, upper, gate_bits, stages),
        out_shape=jax.ShapeDtypeStruct((2 * rows, LANES), jnp.float32),
        in_specs=[pl.BlockSpec(memory_space=pltpu.HBM)] * 4,
        out_specs=pl.BlockSpec(memory_space=pltpu.VMEM),
        scratch_shapes=[
            pltpu.SMEM(gate_qubits.shape, jnp.int32),
            pltpu.SMEM(swap_order.shape, jnp.int32),
            pltpu.VMEM((2 * rows, LANES), jnp.float32),
            pltpu.VMEM(gates.shape, jnp.float32),
            pltpu.VMEM((gate_count + 3, rows, rows), jnp.bfloat16),
            pltpu.VMEM((gate_count, 2 * gate_dim, 2 * gate_dim), jnp.bfloat16),
            pltpu.VMEM((CHUNKS, n_wide, rows // n_wide, LANES), jnp.float32),
            pltpu.VMEM((CHUNKS, n_wide, rows // n_wide, LANES), jnp.float32),
            pltpu.VMEM((CHUNKS, n_narrow, rows // n_narrow, LANES), jnp.float32),
            pltpu.VMEM((CHUNKS, n_narrow, rows // n_narrow, LANES), jnp.float32),
            pltpu.VMEM((1, LANES), jnp.float32),
            pltpu.VMEM((n_wide * n_narrow - 1, 1, LANES), jnp.float32),
            dma((3,)),
            dma((gate_count,)),
            dma((CHUNKS, n_wide - 1)),
            dma((CHUNKS, n_wide - 1)),
            dma((CHUNKS, n_narrow - 1)),
            dma((CHUNKS, n_narrow - 1)),
            dma((n_wide * n_narrow - 1,)),
            dma((n_wide * n_narrow - 1,)),
        ],
        compiler_params=pltpu.CompilerParams(
            collective_id=0, has_side_effects=True, vmem_limit_bytes=67043328
        ),
        name="gate_layers",
    )(gate_qubits, swap_order, woven, gates)
    return final.reshape(rows, 2, LANES).transpose(1, 0, 2).reshape(state.shape)


def solution(mesh):
    in_specs = (P(None, ("wide", "narrow")), P(), P(), P())
    out_specs = P(None, ("wide", "narrow"))
    return jax.shard_map(local, mesh=mesh, in_specs=in_specs, out_specs=out_specs, check_vma=False)
```

profile of v0, /device:TPU:0, one launch (start us, length us, event | category | flops | bytes accessed | tf_op | source)
XLA Modules:
  0.0 38.5 jit_solution(3286320680342627993)
XLA Ops:
  0.0 36.7 %gate_layers.1 = f32[1024,128]{1,0:T(8,128)} custom-call(s32[8,7]{1,0:T(8,128)} %qubits_hbm.1, s32[9]{0:T(128)} %swap_hbm.1, f32[1024,128]{1,0:T(8,128)} %bitcast.11, f32[8,2,128,128]{3,2,1,0:T(8,128)} %gates_ref.1), custom_call_target="tpu_custom_call" | custom-call | tf_op jit(solution)/shard_map/gate_layers/pallas_call | solution.py:297
  36.7 1.9 %copy.8 = f32[2,65536]{1,0:T(2,128)} copy(f32[2,65536]{1,0:T(2,128)} %bitcast.10) | data formatting | bytes 1048576
where the time goes:
time: 38.7 us; the launch traced here: 38.5 us
  Pallas kernels  36.7 us (95%)
  local copies, waits for them, and re-layouts  1.87 us (5%)
    pallas_call x1, Pallas kernels, local(): pl.pallas_call(functools.partial(kernel, n_wide, n_narrow, upper, gate_bi...  36.7 us
    unnamed x1, local copies, waits for them, and re-layouts  1.87 us

commit v1 on v0

--- a/solution.py
+++ b/solution.py
@@ -18,7 +18,7 @@
 MESH = pl.DeviceIdType.MESH
 
 
-def kernel(
+def plain_kernel(
     n_wide,
     n_narrow,
     upper,
@@ -284,7 +284,7 @@
     for_others(lambda apart: ext_copy(apart).wait_send())
 
 
-def local(state, gates, gate_qubits, swap_order):
+def plain_local(state, gates, gate_qubits, swap_order):
     n_wide = lax.axis_size("wide")
     n_narrow = lax.axis_size("narrow")
     upper = state.shape[1].bit_length() - 1 - LANE_QUBITS
@@ -295,7 +295,7 @@
     dma = pltpu.SemaphoreType.DMA
     woven = state.reshape(2, rows, LANES).transpose(1, 0, 2).reshape(2 * rows, LANES)
     final = pl.pallas_call(
-        functools.partial(kernel, n_wide, n_narrow, upper, gate_bits, stages),
+        functools.partial(plain_kernel, n_wide, n_narrow, upper, gate_bits, stages),
         out_shape=jax.ShapeDtypeStruct((2 * rows, LANES), jnp.float32),
         in_specs=[pl.BlockSpec(memory_space=pltpu.HBM)] * 4,
         out_specs=pl.BlockSpec(memory_space=pltpu.VMEM),
@@ -324,8 +324,432 @@
         compiler_params=pltpu.CompilerParams(
             collective_id=0, has_side_effects=True, vmem_limit_bytes=67043328
         ),
+        name="plain_gate_layers",
+    )(gate_qubits, swap_order, woven, gates)
+    return final.reshape(rows, 2, LANES).transpose(1, 0, 2).reshape(state.shape)
+
+
+SIZES = (32, 32, 32, 32)
+GROUPS = ((0,), (1, 2, 3))
+
+
+def kernel(
+    n_wide,
+    n_narrow,
+    upper,
+    gate_bits,
+    stages,
+    sizes,
+    groups,
+    qubits_hbm,
+    swap_hbm,
+    state_ref,
+    gates_ref,
+    out_ref,
+    middle_ref,
+    scale_ref,
+    qubits_ref,
+    swap_ref,
+    state_v,
+    gates_v,
+    perms,
+    mats,
+    turned,
+    wide_out,
+    wide_in,
+    narrow_out,
+    narrow_in,
+    final,
+    ext_out,
+    ext_in,
+    local_sem,
+    gate_sem,
+    wide_send,
+    wide_recv,
+    narrow_send,
+    narrow_recv,
+    ext_send,
+    ext_recv,
+):
+    rows = 2**upper
+    gate_dim = 2**gate_bits
+    rest = rows // gate_dim
+    tiles = rows // LANES
+    narrow_bits = n_narrow.bit_length() - 1
+    wide_me = lax.axis_index("wide")
+    narrow_me = lax.axis_index("narrow")
+    half = LANES // 2
+    chunks = range(len(sizes))
+    starts = [sum(sizes[:k]) for k in chunks]
+    devices = n_wide * n_narrow
+    flat_me = wide_me * n_narrow + narrow_me
+    f32, bf16 = jnp.float32, jnp.bfloat16
+
+    state_copy = pltpu.make_async_copy(state_ref, state_v, local_sem.at[0])
+    state_copy.start()
+    qubits_copy = pltpu.make_async_copy(qubits_hbm, qubits_ref, local_sem.at[1])
+    qubits_copy.start()
+    swap_copy = pltpu.make_async_copy(swap_hbm, swap_ref, local_sem.at[2])
+    swap_copy.start()
+    gate_copies = []
+    for number in range(gates_v.shape[0]):
+        copy = pltpu.make_async_copy(
+            gates_ref.at[number], gates_v.at[number], gate_sem.at[number]
+        )
+        copy.start()
+        gate_copies.append(copy)
+
+    barrier = pltpu.get_barrier_semaphore()
+
+    def device_at(apart):
+        other = lax.rem(flat_me + apart, devices)
+        return (lax.div(other, n_narrow), lax.rem(other, n_narrow))
+
+    for apart in range(1, devices):
+        pl.semaphore_signal(barrier, inc=1, device_id=device_at(apart), device_id_type=MESH)
+
+    def fenced(step):
+        pl.when(flat_me >= 0)(step)
+
+    def gate_layout(number):
+        masks = [jnp.int32(1) << (qubits_ref[number, k] - LANE_QUBITS) for k in range(gate_bits)]
+        left = jnp.int32(rows - 1)
+        for mask in masks:
+            left = left - mask
+        for _ in range(upper - gate_bits):
+            low = left & (-left)
+            masks.append(low)
+            left = left - low
+        return masks
+
+    def swap_layout(order):
+        return [jnp.int32(1) << (swap_ref[k] - LANE_QUBITS) for k in order]
+
+    natural = [jnp.int32(1 << k) for k in range(upper)]
+    column = lax.broadcasted_iota(jnp.int32, (1, rows), 1)
+    row = lax.broadcasted_iota(jnp.int32, (rows, rows), 0)
+    first_half = lax.broadcasted_iota(jnp.int32, (1, LANES), 1) < half
+
+    def make_perm(slot, source, target):
+        index = jnp.zeros((1, rows), jnp.int32)
+        for k in range(upper):
+            index = index + jnp.where((column & (1 << k)) != 0, target[k], 0)
+        place = jnp.zeros((1, rows), jnp.int32)
+        for k in range(upper):
+            place = place + jnp.where((index & source[k]) != 0, 1 << k, 0)
+        perms[slot] = (row == place).astype(f32).astype(bf16)
+
+    def split(values):
+        high = values.astype(bf16)
+        return high, (values - high.astype(f32)).astype(bf16)
+
+    def make_matrix(number):
+        gate_copies[number].wait()
+        real = gates_v[number, 0].T
+        imag = gates_v[number, 1].T
+        whole = jnp.concatenate(
+            [jnp.concatenate([real, imag], axis=1), jnp.concatenate([-imag, real], axis=1)],
+            axis=0,
+        )
+        high, low = split(whole)
+        mats[number, : 2 * gate_dim] = high
+        mats[number, 2 * gate_dim : 4 * gate_dim] = high
+        mats[number, 4 * gate_dim :] = low
+
+    def moved(parts, slot):
+        return jnp.dot(parts, perms[slot], preferred_element_type=f32)
+
+    def gate(parts, slot, number):
+        count = parts.shape[0] // 4
+        parts = moved(parts, slot).astype(bf16)
+
+        def side(first):
+            return jnp.concatenate(
+                [
+                    jnp.concatenate(
+                        [
+                            parts[first : first + count, k * gate_dim : (k + 1) * gate_dim],
+                            parts[first + count : first + 2 * count, k * gate_dim : (k + 1) * gate_dim],
+                        ],
+                        axis=1,
+                    )
+                    for k in range(rest)
+                ],
+                axis=0,
+            )
+
+        high, low = side(0), side(2 * count)
+        mixed = jnp.dot(
+            jnp.concatenate([high, low, high], axis=1), mats[number], preferred_element_type=f32
+        )
+        return jnp.concatenate(
+            [
+                jnp.concatenate(
+                    [
+                        part[k * count : (k + 1) * count, plane * gate_dim : (plane + 1) * gate_dim]
+                        for k in range(rest)
+                    ],
+                    axis=1,
+                )
+                for part in split(mixed)
+                for plane in range(2)
+            ],
+            axis=0,
+        )
+
+    slot = 0
+    plan = []
+    for numbers in stages:
+        plan.append((slot, numbers))
+        slot += len(numbers) + 1
+
+    def prepare(stage, layout, leave):
+        start, numbers = plan[stage]
+        for k, number in enumerate(numbers):
+            target = gate_layout(number)
+            make_perm(start + k, layout, target)
+            make_matrix(number)
+            layout = target
+        make_perm(start + len(numbers), layout, leave)
+
+    def run(parts, stage):
+        start, numbers = plan[stage]
+        for k, number in enumerate(numbers):
+            parts = gate(parts, start + k, number)
+        both = moved(parts, start + len(numbers))
+        count = both.shape[0] // 2
+        return both[:count] + both[count:]
+
+    def wide_copy(chunk, apart):
+        other = lax.rem(wide_me + apart, n_wide)
+        part = pl.ds(starts[chunk], sizes[chunk])
+        return pltpu.make_async_remote_copy(
+            src_ref=wide_out.at[other, part],
+            dst_ref=wide_in.at[wide_me, part],
+            send_sem=wide_send.at[chunk, apart - 1],
+            recv_sem=wide_recv.at[chunk, apart - 1],
+            device_id=(other, narrow_me),
+            device_id_type=MESH,
+        )
+
+    def narrow_copy(chunk, apart):
+        other = lax.rem(narrow_me + apart, n_narrow)
+        part = pl.ds(2 * starts[chunk], 2 * sizes[chunk])
+        return pltpu.make_async_remote_copy(
+            src_ref=narrow_out.at[other, part],
+            dst_ref=narrow_in.at[narrow_me, part],
+            send_sem=narrow_send.at[chunk, apart - 1],
+            recv_sem=narrow_recv.at[chunk, apart - 1],
+            device_id=(wide_me, other),
+            device_id_type=MESH,
+        )
+
+    def ext_copy(apart):
+        return pltpu.make_async_remote_copy(
+            src_ref=ext_out,
+            dst_ref=ext_in.at[apart - 1],
+            send_sem=ext_send.at[apart - 1],
+            recv_sem=ext_recv.at[apart - 1],
+            device_id=device_at(apart),
+            device_id_type=MESH,
+        )
+
+    def first_stage(group):
+        first, count = starts[group[0]], sum(sizes[k] for k in group)
+        parts = jnp.concatenate(
+            [turned[k, first : first + count] for k in range(4)], axis=0
+        )
+        both = run(parts, 0)
+        real, imag = both[:count], both[count:]
+        for m in range(tiles):
+            re, im = real[:, m * LANES : (m + 1) * LANES], imag[:, m * LANES : (m + 1) * LANES]
+            wide_out[2 * m, first : first + count] = jnp.where(
+                first_half, re, pltpu.roll(im, half, 1)
+            )
+            wide_out[2 * m + 1, first : first + count] = jnp.where(
+                first_half, pltpu.roll(re, half, 1), im
+            )
+
+    def first_send(group):
+        first, count = starts[group[0]], sum(sizes[k] for k in group)
+        for chunk in group:
+            for apart in range(1, n_wide):
+                wide_copy(chunk, apart).start()
+        part = pl.ds(first, count)
+        wide_in[wide_me, part] = wide_out[wide_me, part]
+
+    def second_stage(chunk):
+        first, count = starts[chunk], sizes[chunk]
+        for apart in range(1, n_wide):
+            wide_copy(chunk, apart).wait_recv()
+        real, imag = [], []
+        for m in range(tiles):
+            left = wide_in[2 * m, first : first + count]
+            right = wide_in[2 * m + 1, first : first + count]
+            real.append(jnp.where(first_half, left, pltpu.roll(right, half, 1)))
+            imag.append(jnp.where(first_half, pltpu.roll(left, half, 1), right))
+        whole = jnp.concatenate(
+            [jnp.concatenate(real, axis=1), jnp.concatenate(imag, axis=1)], axis=0
+        )
+        both = run(jnp.concatenate(split(whole), axis=0), 1)
+        width = rows // n_narrow
+        for m in range(n_narrow):
+            narrow_out[m, 2 * first : 2 * (first + count)] = both[:, m * width : (m + 1) * width]
+
+    def second_send(chunk):
+        for apart in range(1, n_narrow):
+            narrow_copy(chunk, apart).start()
+        part = pl.ds(2 * starts[chunk], 2 * sizes[chunk])
+        narrow_in[narrow_me, part] = narrow_out[narrow_me, part]
+
+    def third_stage(chunk):
+        first, count = starts[chunk], sizes[chunk]
+        for apart in range(1, n_narrow):
+            narrow_copy(chunk, apart).wait_recv()
+        whole = jnp.concatenate(
+            [narrow_in[m, 2 * first : 2 * (first + count)] for m in range(n_narrow)], axis=1
+        )
+        both = run(jnp.concatenate(split(whole), axis=0), 2)
+        final[0, first : first + count] = both[:count]
+        final[1, first : first + count] = both[count:]
+
+    qubits_copy.wait()
+    prepare_first = functools.partial(prepare, 0, natural)
+    swap_copy.wait()
+    wide_layout = swap_layout(range(upper))
+    narrow_layout = swap_layout(list(range(narrow_bits, upper)) + list(range(narrow_bits)))
+    prepare_first(wide_layout)
+    state_copy.wait()
+    for plane in range(2):
+        high, low = split(state_v[pl.ds(plane, rows, stride=2), :].T)
+        turned[plane] = high
+        turned[2 + plane] = low
+    first_stage(groups[0])
+    pl.semaphore_wait(barrier, devices - 1)
+    first_send(groups[0])
+
+    for group in groups[1:]:
+
+        @fenced
+        def _(group=group):
+            first_stage(group)
+            first_send(group)
+
+    @fenced
+    def _():
+        prepare(1, wide_layout, narrow_layout)
+        prepare(2, narrow_layout, natural)
+
+    last = len(sizes) - 1
+    for chunk in chunks:
+
+        @fenced
+        def _(chunk=chunk):
+            second_stage(chunk)
+            second_send(chunk)
+
+        if chunk > 0:
+
+            @fenced
+            def _(chunk=chunk):
+                third_stage(chunk - 1)
+
+    @fenced
+    def _():
+        third_stage(last)
+        whole = final[...]
+        high, low = whole.max(axis=0), -whole.min(axis=0)
+        high, low = high.max(axis=0, keepdims=True), low.max(axis=0, keepdims=True)
+        for k, value in enumerate((high, low)):
+            value = functools.reduce(
+                jnp.maximum, [value[:, m * LANES : (m + 1) * LANES] for m in range(tiles)]
+            )
+            ext_out[k : k + 1] = value
+        for apart in range(1, devices):
+            ext_copy(apart).start()
+
+    @fenced
+    def _():
+        for plane in range(2):
+            out_ref[pl.ds(plane, rows, stride=2), :] = final[plane].T
+        for chunk in chunks:
+            for apart in range(1, n_wide):
+                wide_copy(chunk, apart).wait_send()
+            for apart in range(1, n_narrow):
+                narrow_copy(chunk, apart).wait_send()
+
+    for apart in range(1, devices):
+        ext_copy(apart).wait_recv()
+    total = jnp.maximum(ext_out[...], ext_in[...].max(axis=0))
+    total = jnp.max(total, axis=1, keepdims=True)
+    highest, lowest = total[0:1], -total[1:2]
+    middle = (highest + lowest) * 0.5
+    halfwidth = (highest - lowest) * 0.5 + 1e-06
+    middle_ref[...] = jnp.broadcast_to(middle, (1, LANES))
+    scale_ref[...] = jnp.broadcast_to(companding / halfwidth, (1, LANES))
+    for apart in range(1, devices):
+        ext_copy(apart).wait_send()
+
+
+def local(state, gates, gate_qubits, swap_order):
+    n_wide = lax.axis_size("wide")
+    n_narrow = lax.axis_size("narrow")
+    upper = state.shape[1].bit_length() - 1 - LANE_QUBITS
+    rows = 2**upper
+    gate_count, gate_bits = gate_qubits.shape
+    gate_dim = 2**gate_bits
+    devices = n_wide * n_narrow
+    if 2 * rows != n_wide * LANES or rows != n_narrow * LANES or gate_dim != LANES:
+        return plain_local(state, gates, gate_qubits, swap_order)
+    stages = (range(3), range(3, 6), range(6, gate_count))
+    dma = pltpu.SemaphoreType.DMA
+    bf16, f32 = jnp.bfloat16, jnp.float32
+    chunks = len(SIZES)
+    woven = state.reshape(2, rows, LANES).transpose(1, 0, 2).reshape(2 * rows, LANES)
+    held = [pltpu.with_memory_space_constraint(x, pltpu.HBM) for x in (gate_qubits, swap_order, woven, gates)]
+    final, middle, scale = pl.pallas_call(
+        functools.partial(kernel, n_wide, n_narrow, upper, gate_bits, stages, SIZES, GROUPS),
+        out_shape=(
+            pltpu.VMEM((2 * rows, LANES), f32),
+            pltpu.VMEM((1, LANES), f32),
+            pltpu.VMEM((1, LANES), f32),
+        ),
+        in_specs=[pl.BlockSpec(memory_space=pltpu.HBM)] * 4,
+        out_specs=[pl.BlockSpec(memory_space=pltpu.VMEM)] * 3,
+        scratch_shapes=[
+            pltpu.SMEM(gate_qubits.shape, jnp.int32),
+            pltpu.SMEM(swap_order.shape, jnp.int32),
+            pltpu.VMEM((2 * rows, LANES), f32),
+            pltpu.VMEM(gates.shape, f32),
+            pltpu.VMEM((gate_count + 3, rows, rows), bf16),
+            pltpu.VMEM((gate_count, 6 * gate_dim, 2 * gate_dim), bf16),
+            pltpu.VMEM((4, LANES, rows), bf16),
+            pltpu.VMEM((n_wide, LANES, LANES), f32),
+            pltpu.VMEM((n_wide, LANES, LANES), f32),
+            pltpu.VMEM((n_narrow, 2 * LANES, LANES), f32),
+            pltpu.VMEM((n_narrow, 2 * LANES, LANES), f32),
+            pltpu.VMEM((2, LANES, rows), f32),
+            pltpu.VMEM((2, LANES), f32),
+            pltpu.VMEM((devices - 1, 2, LANES), f32),
+            dma((3,)),
+            dma((gate_count,)),
+            dma((chunks, n_wide - 1)),
+            dma((chunks, n_wide - 1)),
+            dma((chunks, n_narrow - 1)),
+            dma((chunks, n_narrow - 1)),
+            dma((devices - 1,)),
+            dma((devices - 1,)),
+        ],
+        compiler_params=pltpu.CompilerParams(
+            collective_id=0, has_side_effects=True, vmem_limit_bytes=40000000
+        ),
         name="gate_layers",
-    )(gate_qubits, swap_order, woven, gates)
+    )(*held)
+    values = (final - middle) * scale
+    magnitude = jnp.abs(values)
+    squared = magnitude * magnitude + 1.0
+    grown = jnp.log(magnitude + squared * lax.rsqrt(squared)) * (1.0 / companding_norm)
+    final = jnp.where(values < 0, -grown, grown)
     return final.reshape(rows, 2, LANES).transpose(1, 0, 2).reshape(state.shape)
 
 

time: 38.7 us -> 34.5 us (0.89)
  Pallas kernels: 36.7 us -> 33.3 us
  local copies, waits for them, and re-layouts: 1.87 us -> 0 us
  other arithmetic: 0 us -> 1.04 us
    pallas_call x1, Pallas kernels: 36.7 us -> 33.3 us  [local(): pl.pallas_call(functools.partial(kernel, n_wide, n_narrow, upper, gate_bi...]
    unnamed x1 -> x0, local copies, waits for them, and re-layouts: 1.87 us -> none
    select_n x0 -> x1, other arithmetic: none -> 1.04 us  [local(): final = jnp.where(values < 0, -grown, grown)]
where the time goes in v1:
time: 34.5 us; the launch traced here: 34.4 us
  Pallas kernels  33.3 us (97%)
  other arithmetic  1.04 us (3%)
    pallas_call x1, Pallas kernels, local(): pl.pallas_call(functools.partial(kernel, n_wide, n_narrow, upper, gate_bi...  33.3 us
    select_n x1, other arithmetic, local(): final = jnp.where(values < 0, -grown, grown)  1.04 us

profile of v1, /device:TPU:0, one launch (start us, length us, event | category | flops | bytes accessed | tf_op | source)
XLA Modules:
  0.0 34.4 jit_solution(6305712564423869752)
XLA Ops:
  0.0 33.3 %gate_layers.1 = (f32[1024,128]{1,0:T(8,128)S(1)}, f32[1,128]{1,0:T(1,128)S(1)}, f32[1,128]{1,0:T(1,128)S(1)}) custom-call(s32[8,7]{1,0:T(8,128)} %qubits_hbm.1, s32[9]{0:T(128)} %swap_hbm.1, f32[1024,128]{1,0:T(8,128)} %bitcast.14, f32[8,2,128,128]{3,2,1,0:T(8,128)} %gates_ref.1), custom_call_target="tpu_custom_call" | custom-call | tf_op jit(solution)/shard_map/gate_layers/pallas_call | solution.py:710
  33.3 1.0 %negate_select_fusion = f32[1024,128]{1,0:T(8,128)} fusion(f32[1024,128]{1,0:T(8,128)S(1)} %get-tuple-element.8, f32[128]{0:T(128)S(1)} %bitcast.13, f32[128]{0:T(128)S(1)} %bitcast.12), kind=kLoop, calls=%fused_computation | loop fusion | flops 1441792 | bytes 1049600 | tf_op jit(solution)/shard_map/jit(_where)/select_n | solution.py:752

commit v2 on v1

--- a/solution.py
+++ b/solution.py
@@ -329,8 +329,7 @@
     return final.reshape(rows, 2, LANES).transpose(1, 0, 2).reshape(state.shape)
 
 
-SIZES = (32, 32, 32, 32)
-GROUPS = ((0,), (1, 2, 3))
+CUTS = (64, 64)
 
 
 def kernel(
@@ -340,7 +339,6 @@
     gate_bits,
     stages,
     sizes,
-    groups,
     qubits_hbm,
     swap_hbm,
     state_ref,
@@ -370,6 +368,8 @@
     narrow_recv,
     ext_send,
     ext_recv,
+    wide_ready,
+    narrow_ready,
 ):
     rows = 2**upper
     gate_dim = 2**gate_bits
@@ -382,15 +382,14 @@
     chunks = range(len(sizes))
     starts = [sum(sizes[:k]) for k in chunks]
     devices = n_wide * n_narrow
-    flat_me = wide_me * n_narrow + narrow_me
     f32, bf16 = jnp.float32, jnp.bfloat16
 
-    state_copy = pltpu.make_async_copy(state_ref, state_v, local_sem.at[0])
-    state_copy.start()
     qubits_copy = pltpu.make_async_copy(qubits_hbm, qubits_ref, local_sem.at[1])
     qubits_copy.start()
     swap_copy = pltpu.make_async_copy(swap_hbm, swap_ref, local_sem.at[2])
     swap_copy.start()
+    state_copy = pltpu.make_async_copy(state_ref, state_v, local_sem.at[0])
+    state_copy.start()
     gate_copies = []
     for number in range(gates_v.shape[0]):
         copy = pltpu.make_async_copy(
@@ -401,15 +400,50 @@
 
     barrier = pltpu.get_barrier_semaphore()
 
+    def partners(me, count):
+        found = [me]
+        for k in range(count.bit_length() - 1):
+            step = (1 << k) * (1 - 2 * lax.rem(lax.div(me, 1 << k), 2))
+            found = found + [other + step for other in found]
+        return found
+
+    wide_at = partners(wide_me, n_wide)
+    narrow_at = partners(narrow_me, n_narrow)
+    others = range(1, devices)
+
     def device_at(apart):
-        other = lax.rem(flat_me + apart, devices)
-        return (lax.div(other, n_narrow), lax.rem(other, n_narrow))
-
-    for apart in range(1, devices):
-        pl.semaphore_signal(barrier, inc=1, device_id=device_at(apart), device_id_type=MESH)
-
-    def fenced(step):
-        pl.when(flat_me >= 0)(step)
+        return (wide_at[apart // n_narrow], narrow_at[apart % n_narrow])
+
+    def greet_wide(other, _):
+        pl.semaphore_signal(
+            barrier, inc=1, device_id=(other, narrow_me), device_id_type=MESH
+        )
+
+    def greet_narrow(other, _):
+        pl.semaphore_signal(barrier, inc=1, device_id=(wide_me, other), device_id_type=MESH)
+
+    lax.fori_loop(wide_me + 1, n_wide, greet_wide, None)
+    lax.fori_loop(narrow_me + 1, n_narrow, greet_narrow, None)
+
+    def answer_wide(other, _):
+        pl.semaphore_signal(
+            wide_ready.at[wide_me], inc=1, device_id=(other, narrow_me), device_id_type=MESH
+        )
+        pl.semaphore_signal(wide_ready.at[other], inc=1)
+
+    def answer_narrow(other, _):
+        pl.semaphore_signal(
+            narrow_ready.at[narrow_me], inc=1, device_id=(wide_me, other), device_id_type=MESH
+        )
+        pl.semaphore_signal(narrow_ready.at[other], inc=1)
+
+
+    @pl.when(wide_me + narrow_me > 0)
+    def _():
+        pl.semaphore_wait(barrier, wide_me + narrow_me)
+
+    lax.fori_loop(0, wide_me, answer_wide, None)
+    lax.fori_loop(0, narrow_me, answer_narrow, None)
 
     def gate_layout(number):
         masks = [jnp.int32(1) << (qubits_ref[number, k] - LANE_QUBITS) for k in range(gate_bits)]
@@ -444,20 +478,24 @@
         return high, (values - high.astype(f32)).astype(bf16)
 
     def make_matrix(number):
-        gate_copies[number].wait()
-        real = gates_v[number, 0].T
-        imag = gates_v[number, 1].T
-        whole = jnp.concatenate(
-            [jnp.concatenate([real, imag], axis=1), jnp.concatenate([-imag, real], axis=1)],
-            axis=0,
-        )
-        high, low = split(whole)
-        mats[number, : 2 * gate_dim] = high
-        mats[number, 2 * gate_dim : 4 * gate_dim] = high
-        mats[number, 4 * gate_dim :] = low
+        real = split(gates_v[number, 0].T)
+        imag = split(gates_v[number, 1].T)
+        for k in range(2):
+            top, bottom = 2 * k * gate_dim, (2 * k + 1) * gate_dim
+            mats[number, top:bottom, :gate_dim] = real[k]
+            mats[number, top:bottom, gate_dim:] = imag[k]
+            mats[number, bottom : bottom + gate_dim, :gate_dim] = -imag[k]
+            mats[number, bottom : bottom + gate_dim, gate_dim:] = real[k]
 
     def moved(parts, slot):
-        return jnp.dot(parts, perms[slot], preferred_element_type=f32)
+        middle = rows // 2
+        return jnp.concatenate(
+            [
+                jnp.dot(parts, perms[slot, :, :middle], preferred_element_type=f32),
+                jnp.dot(parts, perms[slot, :, middle:], preferred_element_type=f32),
+            ],
+            axis=1,
+        )
 
     def gate(parts, slot, number):
         count = parts.shape[0] // 4
@@ -479,8 +517,15 @@
             )
 
         high, low = side(0), side(2 * count)
-        mixed = jnp.dot(
-            jnp.concatenate([high, low, high], axis=1), mats[number], preferred_element_type=f32
+        weights = jnp.concatenate([mats[number, : 2 * gate_dim], mats[number]], axis=0)
+        whole = jnp.concatenate([high, low, high], axis=1)
+        middle = whole.shape[0] // 2
+        mixed = jnp.concatenate(
+            [
+                jnp.dot(whole[:middle], weights, preferred_element_type=f32),
+                jnp.dot(whole[middle:], weights, preferred_element_type=f32),
+            ],
+            axis=0,
         )
         return jnp.concatenate(
             [
@@ -521,7 +566,7 @@
         return both[:count] + both[count:]
 
     def wide_copy(chunk, apart):
-        other = lax.rem(wide_me + apart, n_wide)
+        other = wide_at[apart]
         part = pl.ds(starts[chunk], sizes[chunk])
         return pltpu.make_async_remote_copy(
             src_ref=wide_out.at[other, part],
@@ -533,7 +578,7 @@
         )
 
     def narrow_copy(chunk, apart):
-        other = lax.rem(narrow_me + apart, n_narrow)
+        other = narrow_at[apart]
         part = pl.ds(2 * starts[chunk], 2 * sizes[chunk])
         return pltpu.make_async_remote_copy(
             src_ref=narrow_out.at[other, part],
@@ -554,8 +599,8 @@
             device_id_type=MESH,
         )
 
-    def first_stage(group):
-        first, count = starts[group[0]], sum(sizes[k] for k in group)
+    def first_stage(chunk):
+        first, count = starts[chunk], sizes[chunk]
         parts = jnp.concatenate(
             [turned[k, first : first + count] for k in range(4)], axis=0
         )
@@ -570,12 +615,12 @@
                 first_half, pltpu.roll(re, half, 1), im
             )
 
-    def first_send(group):
-        first, count = starts[group[0]], sum(sizes[k] for k in group)
-        for chunk in group:
-            for apart in range(1, n_wide):
-                wide_copy(chunk, apart).start()
-        part = pl.ds(first, count)
+    def first_send(chunk):
+        for apart in range(1, n_wide):
+            if chunk == 0:
+                pl.semaphore_wait(wide_ready.at[wide_at[apart]], 1)
+            wide_copy(chunk, apart).start()
+        part = pl.ds(starts[chunk], sizes[chunk])
         wide_in[wide_me, part] = wide_out[wide_me, part]
 
     def second_stage(chunk):
@@ -598,6 +643,8 @@
 
     def second_send(chunk):
         for apart in range(1, n_narrow):
+            if chunk == 0:
+                pl.semaphore_wait(narrow_ready.at[narrow_at[apart]], 1)
             narrow_copy(chunk, apart).start()
         part = pl.ds(2 * starts[chunk], 2 * sizes[chunk])
         narrow_in[narrow_me, part] = narrow_out[narrow_me, part]
@@ -614,71 +661,53 @@
         final[1, first : first + count] = both[count:]
 
     qubits_copy.wait()
-    prepare_first = functools.partial(prepare, 0, natural)
     swap_copy.wait()
+    state_copy.wait()
+    for number in stages[0]:
+        gate_copies[number].wait()
     wide_layout = swap_layout(range(upper))
     narrow_layout = swap_layout(list(range(narrow_bits, upper)) + list(range(narrow_bits)))
-    prepare_first(wide_layout)
-    state_copy.wait()
+    prepare(0, natural, wide_layout)
     for plane in range(2):
         high, low = split(state_v[pl.ds(plane, rows, stride=2), :].T)
         turned[plane] = high
         turned[2 + plane] = low
-    first_stage(groups[0])
-    pl.semaphore_wait(barrier, devices - 1)
-    first_send(groups[0])
-
-    for group in groups[1:]:
-
-        @fenced
-        def _(group=group):
-            first_stage(group)
-            first_send(group)
-
-    @fenced
-    def _():
-        prepare(1, wide_layout, narrow_layout)
-        prepare(2, narrow_layout, natural)
+    for chunk in chunks:
+        first_stage(chunk)
+        first_send(chunk)
+
+    for number in range(stages[1][0], gates_v.shape[0]):
+        gate_copies[number].wait()
+    prepare(1, wide_layout, narrow_layout)
+    prepare(2, narrow_layout, natural)
 
     last = len(sizes) - 1
     for chunk in chunks:
-
-        @fenced
-        def _(chunk=chunk):
-            second_stage(chunk)
-            second_send(chunk)
-
+        second_stage(chunk)
+        second_send(chunk)
         if chunk > 0:
-
-            @fenced
-            def _(chunk=chunk):
-                third_stage(chunk - 1)
-
-    @fenced
-    def _():
-        third_stage(last)
-        whole = final[...]
-        high, low = whole.max(axis=0), -whole.min(axis=0)
-        high, low = high.max(axis=0, keepdims=True), low.max(axis=0, keepdims=True)
-        for k, value in enumerate((high, low)):
-            value = functools.reduce(
-                jnp.maximum, [value[:, m * LANES : (m + 1) * LANES] for m in range(tiles)]
-            )
-            ext_out[k : k + 1] = value
-        for apart in range(1, devices):
-            ext_copy(apart).start()
-
-    @fenced
-    def _():
-        for plane in range(2):
-            out_ref[pl.ds(plane, rows, stride=2), :] = final[plane].T
-        for chunk in chunks:
-            for apart in range(1, n_wide):
-                wide_copy(chunk, apart).wait_send()
-            for apart in range(1, n_narrow):
-                narrow_copy(chunk, apart).wait_send()
-
-    for apart in range(1, devices):
+            third_stage(chunk - 1)
+    third_stage(last)
+
+    whole = final[...]
+    high, low = whole.max(axis=0), -whole.min(axis=0)
+    for k, value in enumerate((high, low)):
+        value = value.max(axis=0, keepdims=True)
+        ext_out[k : k + 1] = functools.reduce(
+            jnp.maximum, [value[:, m * LANES : (m + 1) * LANES] for m in range(tiles)]
+        )
+    for apart in others:
+        ext_copy(apart).start()
+
+    for plane in range(2):
+        out_ref[pl.ds(plane, rows, stride=2), :] = final[plane].T
+    for chunk in chunks:
+        for apart in range(1, n_wide):
+            wide_copy(chunk, apart).wait_send()
+        for apart in range(1, n_narrow):
+            narrow_copy(chunk, apart).wait_send()
+
+    for apart in others:
         ext_copy(apart).wait_recv()
     total = jnp.maximum(ext_out[...], ext_in[...].max(axis=0))
     total = jnp.max(total, axis=1, keepdims=True)
@@ -687,7 +716,7 @@
     halfwidth = (highest - lowest) * 0.5 + 1e-06
     middle_ref[...] = jnp.broadcast_to(middle, (1, LANES))
     scale_ref[...] = jnp.broadcast_to(companding / halfwidth, (1, LANES))
-    for apart in range(1, devices):
+    for apart in others:
         ext_copy(apart).wait_send()
 
 
@@ -704,11 +733,15 @@
     stages = (range(3), range(3, 6), range(6, gate_count))
     dma = pltpu.SemaphoreType.DMA
     bf16, f32 = jnp.bfloat16, jnp.float32
-    chunks = len(SIZES)
+    sizes = [cut * LANES // sum(CUTS) for cut in CUTS]
+    chunks = len(sizes)
     woven = state.reshape(2, rows, LANES).transpose(1, 0, 2).reshape(2 * rows, LANES)
-    held = [pltpu.with_memory_space_constraint(x, pltpu.HBM) for x in (gate_qubits, swap_order, woven, gates)]
+    held = [
+        pltpu.with_memory_space_constraint(x, pltpu.HBM)
+        for x in (gate_qubits, swap_order, woven, gates)
+    ]
     final, middle, scale = pl.pallas_call(
-        functools.partial(kernel, n_wide, n_narrow, upper, gate_bits, stages, SIZES, GROUPS),
+        functools.partial(kernel, n_wide, n_narrow, upper, gate_bits, stages, sizes),
         out_shape=(
             pltpu.VMEM((2 * rows, LANES), f32),
             pltpu.VMEM((1, LANES), f32),
@@ -722,7 +755,7 @@
             pltpu.VMEM((2 * rows, LANES), f32),
             pltpu.VMEM(gates.shape, f32),
             pltpu.VMEM((gate_count + 3, rows, rows), bf16),
-            pltpu.VMEM((gate_count, 6 * gate_dim, 2 * gate_dim), bf16),
+            pltpu.VMEM((gate_count, 4 * gate_dim, 2 * gate_dim), bf16),
             pltpu.VMEM((4, LANES, rows), bf16),
             pltpu.VMEM((n_wide, LANES, LANES), f32),
             pltpu.VMEM((n_wide, LANES, LANES), f32),
@@ -739,6 +772,8 @@
             dma((chunks, n_narrow - 1)),
             dma((devices - 1,)),
             dma((devices - 1,)),
+            pltpu.SemaphoreType.REGULAR((n_wide,)),
+            pltpu.SemaphoreType.REGULAR((n_narrow,)),
         ],
         compiler_params=pltpu.CompilerParams(
             collective_id=0, has_side_effects=True, vmem_limit_bytes=40000000

time: 34.5 us -> 32.7 us (0.948)
  Pallas kernels: 33.3 us -> 31.5 us
    pallas_call x1, Pallas kernels: 33.3 us -> 31.5 us  [local(): pl.pallas_call(functools.partial(kernel, n_wide, n_narrow, upper, gate_bi...]
where the time goes in v2:
time: 32.7 us; the launch traced here: 32.6 us
  Pallas kernels  31.5 us (96%)
  other arithmetic  1.04 us (3%)
    pallas_call x1, Pallas kernels, local(): pl.pallas_call(functools.partial(kernel, n_wide, n_narrow, upper, gate_bi...  31.5 us
    select_n x1, other arithmetic, local(): final = jnp.where(values < 0, -grown, grown)  1.04 us

profile of v2, /device:TPU:0, one launch (start us, length us, event | category | flops | bytes accessed | tf_op | source)
XLA Modules:
  0.0 32.6 jit_solution(8514090087534830363)
XLA Ops:
  0.0 31.5 %gate_layers.1 = (f32[1024,128]{1,0:T(8,128)S(1)}, f32[1,128]{1,0:T(1,128)S(1)}, f32[1,128]{1,0:T(1,128)S(1)}) custom-call(s32[8,7]{1,0:T(8,128)} %qubits_hbm.1, s32[9]{0:T(128)} %swap_hbm.1, f32[1024,128]{1,0:T(8,128)} %bitcast.14, f32[8,2,128,128]{3,2,1,0:T(8,128)} %gates_ref.1), custom_call_target="tpu_custom_call" | custom-call | tf_op jit(solution)/shard_map/gate_layers/pallas_call | solution.py:743
  31.5 1.0 %negate_select_fusion = f32[1024,128]{1,0:T(8,128)} fusion(f32[1024,128]{1,0:T(8,128)S(1)} %get-tuple-element.8, f32[128]{0:T(128)S(1)} %bitcast.13, f32[128]{0:T(128)S(1)} %bitcast.12), kind=kLoop, calls=%fused_computation | loop fusion | flops 1441792 | bytes 1049600 | tf_op jit(solution)/shard_map/jit(_where)/select_n | solution.py:787

commit v3 on v2

--- a/solution.py
+++ b/solution.py
@@ -361,7 +361,6 @@
     ext_out,
     ext_in,
     local_sem,
-    gate_sem,
     wide_send,
     wide_recv,
     narrow_send,
@@ -390,13 +389,15 @@
     swap_copy.start()
     state_copy = pltpu.make_async_copy(state_ref, state_v, local_sem.at[0])
     state_copy.start()
-    gate_copies = []
-    for number in range(gates_v.shape[0]):
-        copy = pltpu.make_async_copy(
-            gates_ref.at[number], gates_v.at[number], gate_sem.at[number]
-        )
+    soon = len(stages[0])
+    gate_copies = [
+        pltpu.make_async_copy(
+            gates_ref.at[first:after], gates_v.at[first:after], local_sem.at[3 + k]
+        )
+        for k, (first, after) in enumerate(((0, soon), (soon, gates_v.shape[0])))
+    ]
+    for copy in gate_copies:
         copy.start()
-        gate_copies.append(copy)
 
     barrier = pltpu.get_barrier_semaphore()
 
@@ -409,7 +410,7 @@
 
     wide_at = partners(wide_me, n_wide)
     narrow_at = partners(narrow_me, n_narrow)
-    others = range(1, devices)
+    others = range(devices - 1, 0, -1)
 
     def device_at(apart):
         return (wide_at[apart // n_narrow], narrow_at[apart % n_narrow])
@@ -461,7 +462,7 @@
 
     natural = [jnp.int32(1 << k) for k in range(upper)]
     column = lax.broadcasted_iota(jnp.int32, (1, rows), 1)
-    row = lax.broadcasted_iota(jnp.int32, (rows, rows), 0)
+    row = lax.broadcasted_iota(jnp.int32, (rows, rows), 0).astype(jnp.int16)
     first_half = lax.broadcasted_iota(jnp.int32, (1, LANES), 1) < half
 
     def make_perm(slot, source, target):
@@ -471,7 +472,7 @@
         place = jnp.zeros((1, rows), jnp.int32)
         for k in range(upper):
             place = place + jnp.where((index & source[k]) != 0, 1 << k, 0)
-        perms[slot] = (row == place).astype(f32).astype(bf16)
+        perms[slot] = jnp.where(row == place.astype(jnp.int16), bf16(1), bf16(0))
 
     def split(values):
         high = values.astype(bf16)
@@ -571,8 +572,8 @@
         return pltpu.make_async_remote_copy(
             src_ref=wide_out.at[other, part],
             dst_ref=wide_in.at[wide_me, part],
-            send_sem=wide_send.at[chunk, apart - 1],
-            recv_sem=wide_recv.at[chunk, apart - 1],
+            send_sem=wide_send.at[chunk],
+            recv_sem=wide_recv.at[chunk],
             device_id=(other, narrow_me),
             device_id_type=MESH,
         )
@@ -583,8 +584,8 @@
         return pltpu.make_async_remote_copy(
             src_ref=narrow_out.at[other, part],
             dst_ref=narrow_in.at[narrow_me, part],
-            send_sem=narrow_send.at[chunk, apart - 1],
-            recv_sem=narrow_recv.at[chunk, apart - 1],
+            send_sem=narrow_send.at[chunk],
+            recv_sem=narrow_recv.at[chunk],
             device_id=(wide_me, other),
             device_id_type=MESH,
         )
@@ -593,11 +594,22 @@
         return pltpu.make_async_remote_copy(
             src_ref=ext_out,
             dst_ref=ext_in.at[apart - 1],
-            send_sem=ext_send.at[apart - 1],
-            recv_sem=ext_recv.at[apart - 1],
+            send_sem=ext_send.at[0],
+            recv_sem=ext_recv.at[0],
             device_id=device_at(apart),
             device_id_type=MESH,
         )
+
+    def await_wide(chunk, sems):
+        all_of = wide_in.at[: n_wide - 1, pl.ds(starts[chunk], sizes[chunk])]
+        pltpu.make_async_copy(all_of, all_of, sems.at[chunk]).wait()
+
+    def await_narrow(chunk, sems):
+        all_of = narrow_in.at[: n_narrow - 1, pl.ds(2 * starts[chunk], 2 * sizes[chunk])]
+        pltpu.make_async_copy(all_of, all_of, sems.at[chunk]).wait()
+
+    def await_ext(sems):
+        pltpu.make_async_copy(ext_in, ext_in, sems.at[0]).wait()
 
     def first_stage(chunk):
         first, count = starts[chunk], sizes[chunk]
@@ -625,8 +637,7 @@
 
     def second_stage(chunk):
         first, count = starts[chunk], sizes[chunk]
-        for apart in range(1, n_wide):
-            wide_copy(chunk, apart).wait_recv()
+        await_wide(chunk, wide_recv)
         real, imag = [], []
         for m in range(tiles):
             left = wide_in[2 * m, first : first + count]
@@ -651,8 +662,7 @@
 
     def third_stage(chunk):
         first, count = starts[chunk], sizes[chunk]
-        for apart in range(1, n_narrow):
-            narrow_copy(chunk, apart).wait_recv()
+        await_narrow(chunk, narrow_recv)
         whole = jnp.concatenate(
             [narrow_in[m, 2 * first : 2 * (first + count)] for m in range(n_narrow)], axis=1
         )
@@ -663,8 +673,7 @@
     qubits_copy.wait()
     swap_copy.wait()
     state_copy.wait()
-    for number in stages[0]:
-        gate_copies[number].wait()
+    gate_copies[0].wait()
     wide_layout = swap_layout(range(upper))
     narrow_layout = swap_layout(list(range(narrow_bits, upper)) + list(range(narrow_bits)))
     prepare(0, natural, wide_layout)
@@ -676,8 +685,7 @@
         first_stage(chunk)
         first_send(chunk)
 
-    for number in range(stages[1][0], gates_v.shape[0]):
-        gate_copies[number].wait()
+    gate_copies[1].wait()
     prepare(1, wide_layout, narrow_layout)
     prepare(2, narrow_layout, natural)
 
@@ -699,16 +707,15 @@
     for apart in others:
         ext_copy(apart).start()
 
-    for plane in range(2):
+    def weave(plane, _):
         out_ref[pl.ds(plane, rows, stride=2), :] = final[plane].T
+
+    lax.fori_loop(0, 2, weave, None)
     for chunk in chunks:
-        for apart in range(1, n_wide):
-            wide_copy(chunk, apart).wait_send()
-        for apart in range(1, n_narrow):
-            narrow_copy(chunk, apart).wait_send()
-
-    for apart in others:
-        ext_copy(apart).wait_recv()
+        await_wide(chunk, wide_send)
+        await_narrow(chunk, narrow_send)
+
+    await_ext(ext_recv)
     total = jnp.maximum(ext_out[...], ext_in[...].max(axis=0))
     total = jnp.max(total, axis=1, keepdims=True)
     highest, lowest = total[0:1], -total[1:2]
@@ -716,8 +723,7 @@
     halfwidth = (highest - lowest) * 0.5 + 1e-06
     middle_ref[...] = jnp.broadcast_to(middle, (1, LANES))
     scale_ref[...] = jnp.broadcast_to(companding / halfwidth, (1, LANES))
-    for apart in others:
-        ext_copy(apart).wait_send()
+    await_ext(ext_send)
 
 
 def local(state, gates, gate_qubits, swap_order):
@@ -764,14 +770,13 @@
             pltpu.VMEM((2, LANES, rows), f32),
             pltpu.VMEM((2, LANES), f32),
             pltpu.VMEM((devices - 1, 2, LANES), f32),
-            dma((3,)),
-            dma((gate_count,)),
-            dma((chunks, n_wide - 1)),
-            dma((chunks, n_wide - 1)),
-            dma((chunks, n_narrow - 1)),
-            dma((chunks, n_narrow - 1)),
-            dma((devices - 1,)),
-            dma((devices - 1,)),
+            dma((5,)),
+            dma((chunks,)),
+            dma((chunks,)),
+            dma((chunks,)),
+            dma((chunks,)),
+            dma((1,)),
+            dma((1,)),
             pltpu.SemaphoreType.REGULAR((n_wide,)),
             pltpu.SemaphoreType.REGULAR((n_narrow,)),
         ],

time: 32.7 us -> 31.5 us (0.963)
  Pallas kernels: 31.5 us -> 30.3 us
    pallas_call x1, Pallas kernels: 31.5 us -> 30.3 us  [local(): pl.pallas_call(functools.partial(kernel, n_wide, n_narrow, upper, gate_bi...]
where the time goes in v3:
time: 31.5 us; the launch traced here: 31.3 us
  Pallas kernels  30.3 us (96%)
  other arithmetic  1.04 us (3%)
    pallas_call x1, Pallas kernels, local(): pl.pallas_call(functools.partial(kernel, n_wide, n_narrow, upper, gate_bi...  30.3 us
    select_n x1, other arithmetic, local(): final = jnp.where(values < 0, -grown, grown)  1.04 us

profile of v3, /device:TPU:0, one launch (start us, length us, event | category | flops | bytes accessed | tf_op | source)
XLA Modules:
  0.0 31.3 jit_solution(17371034799374193267)
XLA Ops:
  0.0 30.3 %gate_layers.1 = (f32[1024,128]{1,0:T(8,128)S(1)}, f32[1,128]{1,0:T(1,128)S(1)}, f32[1,128]{1,0:T(1,128)S(1)}) custom-call(s32[8,7]{1,0:T(8,128)} %qubits_hbm.1, s32[9]{0:T(128)} %swap_hbm.1, f32[1024,128]{1,0:T(8,128)} %bitcast.14, f32[8,2,128,128]{3,2,1,0:T(8,128)} %gates_ref.1), custom_call_target="tpu_custom_call" | custom-call | tf_op jit(solution)/shard_map/gate_layers/pallas_call | solution.py:749
  30.3 1.0 %negate_select_fusion = f32[1024,128]{1,0:T(8,128)} fusion(f32[1024,128]{1,0:T(8,128)S(1)} %get-tuple-element.8, f32[128]{0:T(128)S(1)} %bitcast.13, f32[128]{0:T(128)S(1)} %bitcast.12), kind=kLoop, calls=%fused_computation | loop fusion | flops 1441792 | bytes 1049600 | tf_op jit(solution)/shard_map/jit(_where)/select_n | solution.py:792

commit v4 on v3

--- a/solution.py
+++ b/solution.py
@@ -410,10 +410,7 @@
 
     wide_at = partners(wide_me, n_wide)
     narrow_at = partners(narrow_me, n_narrow)
-    others = range(devices - 1, 0, -1)
-
-    def device_at(apart):
-        return (wide_at[apart // n_narrow], narrow_at[apart % n_narrow])
+    flat_me = wide_me * n_narrow + narrow_me
 
     def greet_wide(other, _):
         pl.semaphore_signal(
@@ -590,13 +587,14 @@
             device_id_type=MESH,
         )
 
-    def ext_copy(apart):
+    def ext_copy(place):
+        other = place + lax.div(place + devices - flat_me, devices)
         return pltpu.make_async_remote_copy(
             src_ref=ext_out,
-            dst_ref=ext_in.at[apart - 1],
+            dst_ref=ext_in.at[flat_me],
             send_sem=ext_send.at[0],
             recv_sem=ext_recv.at[0],
-            device_id=device_at(apart),
+            device_id=(lax.div(other, n_narrow), lax.rem(other, n_narrow)),
             device_id_type=MESH,
         )
 
@@ -609,7 +607,8 @@
         pltpu.make_async_copy(all_of, all_of, sems.at[chunk]).wait()
 
     def await_ext(sems):
-        pltpu.make_async_copy(ext_in, ext_in, sems.at[0]).wait()
+        all_of = ext_in.at[: devices - 1]
+        pltpu.make_async_copy(all_of, all_of, sems.at[0]).wait()
 
     def first_stage(chunk):
         first, count = starts[chunk], sizes[chunk]
@@ -704,8 +703,9 @@
         ext_out[k : k + 1] = functools.reduce(
             jnp.maximum, [value[:, m * LANES : (m + 1) * LANES] for m in range(tiles)]
         )
-    for apart in others:
-        ext_copy(apart).start()
+    for place in range(devices - 1):
+        ext_copy(place).start()
+    ext_in[flat_me] = ext_out[...]
 
     def weave(plane, _):
         out_ref[pl.ds(plane, rows, stride=2), :] = final[plane].T
@@ -716,7 +716,7 @@
         await_narrow(chunk, narrow_send)
 
     await_ext(ext_recv)
-    total = jnp.maximum(ext_out[...], ext_in[...].max(axis=0))
+    total = ext_in[...].max(axis=0)
     total = jnp.max(total, axis=1, keepdims=True)
     highest, lowest = total[0:1], -total[1:2]
     middle = (highest + lowest) * 0.5
@@ -769,7 +769,7 @@
             pltpu.VMEM((n_narrow, 2 * LANES, LANES), f32),
             pltpu.VMEM((2, LANES, rows), f32),
             pltpu.VMEM((2, LANES), f32),
-            pltpu.VMEM((devices - 1, 2, LANES), f32),
+            pltpu.VMEM((devices, 2, LANES), f32),
             dma((5,)),
             dma((chunks,)),
             dma((chunks,)),

time: 31.5 us -> 31.4 us (level)
  no operation moved by 1% of the time
where the time goes in v4:
time: 31.4 us; the launch traced here: 31.2 us
  Pallas kernels  30.2 us (96%)
  other arithmetic  1.04 us (3%)
    pallas_call x1, Pallas kernels, local(): pl.pallas_call(functools.partial(kernel, n_wide, n_narrow, upper, gate_bi...  30.2 us
    select_n x1, other arithmetic, local(): final = jnp.where(values < 0, -grown, grown)  1.04 us

profile of v4, /device:TPU:0, one launch (start us, length us, event | category | flops | bytes accessed | tf_op | source)
XLA Modules:
  0.0 31.2 jit_solution(11744633562553245954)
XLA Ops:
  0.0 30.2 %gate_layers.1 = (f32[1024,128]{1,0:T(8,128)S(1)}, f32[1,128]{1,0:T(1,128)S(1)}, f32[1,128]{1,0:T(1,128)S(1)}) custom-call(s32[8,7]{1,0:T(8,128)} %qubits_hbm.1, s32[9]{0:T(128)} %swap_hbm.1, f32[1024,128]{1,0:T(8,128)} %bitcast.14, f32[8,2,128,128]{3,2,1,0:T(8,128)} %gates_ref.1), custom_call_target="tpu_custom_call" | custom-call | tf_op jit(solution)/shard_map/gate_layers/pallas_call | solution.py:749
  30.2 1.0 %negate_select_fusion = f32[1024,128]{1,0:T(8,128)} fusion(f32[1024,128]{1,0:T(8,128)S(1)} %get-tuple-element.8, f32[128]{0:T(128)S(1)} %bitcast.13, f32[128]{0:T(128)S(1)} %bitcast.12), kind=kLoop, calls=%fused_computation | loop fusion | flops 1441792 | bytes 1049600 | tf_op jit(solution)/shard_map/jit(_where)/select_n | solution.py:792
